TPU v7x, 32 devices: a whole 2x2x4 slice. The times are simulated.
32 devices in a mesh: frames: 2 (over y), az: 8 (over z, x), rg: 2 (over core).
Axes of the slice: x: 2, y: 2, z: 4, core: 2. Of those that a mesh axis runs over, the one named last changes fastest.
Arguments:
- raw: bfloat16 [2, 512, 8, 2048], P(None, ('frames', 'az'), None, 'rg'), parts along dimension 1, may hold values from -6 to 6
- stolt_weights: bfloat16 [4, 16, 256, 128], P(None, 'rg'), may hold values from -0.375 to 0.375
- band_start: int32 [4, 16], replicated, may hold values from 0 to 14, as said below
Outputs:
- image: bfloat16 [2, 512, 8, 2048], P(None, ('frames', 'az'), None, 'rg'), parts along dimension 1
There are 2 independent parts, one for each index of `frames`. A program takes and returns all parts, laid end to end along the dimension named above; an argument that names none is the same for every part. Nothing has to cross between parts.
Inputs may be any that keep to these rules, and one draw needn't show every extreme that they name: band_start[g, j] is (j) - 1 or (j), clipped to the range; for every block j from 1 to 14 some slab has (j) - 1 and some slab has (j).
All inputs are finite; a program needn't handle non-finite values.
Results may differ from a plain program's by a relative error of at most 0.001.
Values may be sent and summed in bfloat16 or wider, within the bound.
No kernel may reach another device: no remote copies, remote signals or barrier semaphores. Data moves between devices by JAX's collectives and lax.ppermute only.
A program may use at most 64 MiB of HBM per device.

v0:
```python
import math
import jax
import jax.numpy as jnp
from jax import lax
from jax.sharding import PartitionSpec as P

LINES_DEV = 256
SLABS = 4


def with_halo(cells, sides, width):
    for axis, dim in sides:
        count = lax.axis_size(axis)
        ends = count - 1
        head = lax.slice_in_dim(cells, 0, width, axis=dim)
        tail = lax.slice_in_dim(cells, cells.shape[dim] - width, cells.shape[dim], axis=dim)
        cells = jnp.concatenate(
            [
                lax.ppermute(tail, axis, [(i, (i + 1) % count) for i in range(ends)]),
                cells,
                lax.ppermute(head, axis, [((i + 1) % count, i) for i in range(ends)]),
            ],
            axis=dim,
        )
    return cells


def dft_table(length, direction, factor):
    counter = jnp.arange(length, dtype=jnp.int32)
    product = counter[:, None] * counter[None, :] % length
    angles = product.astype(jnp.float32) * (2.0 * math.pi / length)
    cosine = jnp.cos(angles) * factor
    sines = jnp.sin(angles) * (factor * direction)
    return jnp.stack([jnp.stack([cosine, -sines], 1), jnp.stack([sines, cosine], 1)], 0)


def rotate(real_part, imag_part, phase_index, line_total, direction):
    angles = phase_index.astype(jnp.float32) * (2.0 * math.pi / line_total)
    cosine = jnp.cos(angles)
    sines = jnp.sin(angles) * direction
    return (real_part * cosine - imag_part * sines, imag_part * cosine + real_part * sines)


def stolt(slab_source, weights, starts, slab_rows):
    pieces = []
    for slab_index in range(weights.shape[0]):
        slab_data = slab_source[:, slab_index * slab_rows : (slab_index + 1) * slab_rows, :]

        def window_at(start_bin):
            return lax.dynamic_slice_in_dim(slab_data, start_bin, 256, 2)

        windows = jax.vmap(window_at)(starts[slab_index])
        remixed = jnp.einsum(
            "jcmb,jbo->cmjo",
            windows,
            weights[slab_index].astype(jnp.float32),
            precision=lax.Precision.HIGHEST,
        )
        pieces.append(remixed.reshape(2, slab_rows, -1))
    return jnp.concatenate(pieces, 1)


def body(raw, stolt_weights, band_start):
    groups = lax.axis_size("az")
    az_index = lax.axis_index("az")
    rg_index = lax.axis_index("rg")
    part_lines = raw.shape[1]
    bin_count = raw.shape[3]
    line_total = LINES_DEV * groups
    short_forward = dft_table(groups, -1.0, 1.0 / math.sqrt(groups))
    spread = jnp.einsum(
        "dkcp,cmpr->dmkr", short_forward, raw.astype(jnp.float32), precision=lax.Precision.HIGHEST
    )
    line_index = az_index * part_lines + jnp.arange(part_lines, dtype=jnp.int32)
    freq_index = jnp.arange(groups, dtype=jnp.int32)
    phase_index = line_index[:, None] * freq_index[None, :] % line_total
    real_part, imag_part = rotate(spread[0], spread[1], phase_index[:, :, None], line_total, -1.0)
    twisted = jnp.stack([real_part, imag_part])
    long_forward = dft_table(LINES_DEV, -1.0, 1.0 / math.sqrt(LINES_DEV))
    spectrum = jnp.einsum(
        "dkcm,cmjr->dkjr",
        long_forward,
        lax.all_to_all(twisted, "az", split_axis=2, concat_axis=1, tiled=True),
        precision=lax.Precision.HIGHEST,
    )
    spectrum_rows = spectrum[:, :, 0, :]
    slab_rows = LINES_DEV // SLABS
    block_count = bin_count // 128
    padded = with_halo(spectrum_rows, (("rg", 2),), 128)
    local_band = lax.dynamic_slice_in_dim(band_start, rg_index * block_count, block_count, 1)
    starts = (local_band - rg_index * block_count) * 128 + 128
    remapped = stolt(padded, stolt_weights, starts, slab_rows)
    long_inverse = dft_table(LINES_DEV, 1.0, 1.0 / math.sqrt(LINES_DEV))
    lines_back = jnp.einsum(
        "dmck,ckr->dmr", long_inverse, remapped, precision=lax.Precision.HIGHEST
    )
    all_lines = jnp.arange(LINES_DEV, dtype=jnp.int32)
    back_index = all_lines * az_index % line_total
    real_part, imag_part = rotate(
        lines_back[0], lines_back[1], back_index[:, None], line_total, 1.0
    )
    unrolled = jnp.stack([real_part, imag_part])[:, :, None, :]
    short_inverse = dft_table(groups, 1.0, 1.0 / math.sqrt(groups))
    focused = jnp.einsum(
        "dpck,cmkr->dmpr",
        short_inverse,
        lax.all_to_all(unrolled, "az", split_axis=1, concat_axis=2, tiled=True),
        precision=lax.Precision.HIGHEST,
    )
    return focused.astype(jnp.bfloat16)


def solution(mesh):
    placed = (P(None, ("frames", "az"), None, "rg"), P(None, "rg", None, None), P())
    return jax.shard_map(
        body,
        mesh=mesh,
        in_specs=placed,
        out_specs=P(None, ("frames", "az"), None, "rg"),
        check_vma=False,
    )
```

profile of v0, /device:TPU:0, one launch (start us, length us, event | category | flops | bytes accessed | tf_op | source)
XLA Modules:
  0.0 164.7 jit_solution(4455382401302081138)
XLA Ops:
  0.0 0.1 cosine_multiply_fusion.1
  0.1 0.1 broadcast_multiply_fusion.3
  0.1 0.1 fusion.88
  0.2 0.2 fusion.79
  0.4 2.3 %convolution_bitcast_fusion.1 = f32[2,32,8,1024]{3,2,1,0:T(8,128)S(1)} fusion(bf16[2,32,8,1024]{3,2,1,0:T(8,128)(2,1)} %param.3, f32[1,8,2,8]{3,1,2,0:T(8,128)S(1)} %get-tuple-element.21, f32[1,8,2,8]{3,1,2,0:T(8,128)S(1)} %get-tuple-element.22), kind=kOutput, calls=%fused_computation.29 | convolution fusion | flops 100663552 | bytes 3146752 | tf_op jit(solution)/shard_map/dkcp,cmpr->dmkr/dot_general | solution.py:71
  2.6 0.3 multiply_subtract_fusion.1
  2.9 0.2 pad_maximum_fusion.1
  3.2 2.6 %copy.49 = f32[2,32,8,1024]{3,1,0,2:T(8,128)} copy(f32[2,32,8,1024]{3,2,1,0:T(8,128)S(1)} %pad_maximum_fusion.1) | data formatting | bytes 4194304 | tf_op jit(solution)/shard_map/stack | solution.py:78
  5.7 7.3 %all-to-all-start = ((f32[2,32,8,1024]{3,1,0,2:T(8,128)}), f32[2,32,8,1024]{3,1,0,2:T(8,128)S(1)}, u32[]{:S(2)}, u32[]{:S(2)}) async-start(f32[2,32,8,1024]{3,1,0,2:T(8,128)} %copy.49), calls=%async_computation | async-start | bytes 4194304 | tf_op jit(solution)/shard_map/all_to_all | solution.py:83
  13.0 0.1 fusion.104
  13.0 1.0 fusion.64
  14.0 1.1 cosine_multiply_fusion
  15.1 1.0 broadcast_multiply_fusion.1
  16.1 1.2 fusion.46
  17.2 44.0 %all-to-all-done = f32[2,32,8,1024]{3,1,0,2:T(8,128)S(1)} async-done(((f32[2,32,8,1024]{3,1,0,2:T(8,128)}), f32[2,32,8,1024]{3,1,0,2:T(8,128)S(1)}, u32[]{:S(2)}, u32[]{:S(2)}) %all-to-all-start) | async-done | bytes 2097184 | tf_op jit(solution)/shard_map/all_to_all | solution.py:83
  61.2 0.1 copy.50
  61.4 0.0 copy-start.5
  61.4 3.6 %convolution_bitcast_fusion = f32[2,256,1024]{2,1,0:T(8,128)S(1)} fusion(f32[2,256,1024,1]{2,1,0,3:T(8,128)S(1)} %bitcast.139, f32[1,256,2,256]{3,1,2,0:T(8,128)S(1)} %get-tuple-element.16, f32[1,256,2,256]{3,1,2,0:T(8,128)S(1)} %get-tuple-element.17), kind=kOutput, calls=%fused_computation.28 | convolution fusion | flops 3221487616 | bytes 5242880 | tf_op jit(solution)/shard_map/dkcm,cmjr->dkjr/dot_general | solution.py:80
  65.0 1.3 collective-permute-start
  66.3 1.3 collective-permute-start.1
  67.6 0.1 multiply_add_fusion.2
  67.7 0.0 collective-permute-done
  67.8 2.0 %collective-permute-done.1 = f32[2,256,128]{2,1,0:T(8,128)S(1)} collective-permute-done((f32[2,256,128]{2,1,0:T(8,128)S(1)}, f32[2,256,128]{2,1,0:T(8,128)S(1)}, u32[]{:S(2)}, u32[]{:S(2)}) %collective-permute-start.1) | collective-permute-done | bytes 262176 | tf_op jit(solution)/shard_map/ppermute | solution.py:21
  69.8 0.2 pad_maximum_fusion
  70.0 1.3 fusion.110
  71.3 0.7 copy.57
  71.9 2.8 %gather_fusion.2 = f32[8,2,64,256]{2,1,3,0:T(2,128)S(1)} fusion(f32[2,64,1280]{1,0,2:T(2,128)S(1)} %copy.57, s32[8]{0:T(128)S(1)} %get-tuple-element.25), kind=kCustom, calls=%fused_computation.2 | custom fusion | bytes 2097248 | tf_op jit(solution)/shard_map/vmap()/gather | solution.py:50
  74.7 2.9 %fusion.30 = f32[8,2,8,8,128]{4,3,2,1,0:T(8,128)S(1)} fusion(f32[8,2,64,256]{2,1,3,0:T(2,128)S(1)} %gather_fusion.2, bf16[4,8,256,128]{3,2,1,0:T(8,128)(2,1)} %param.4), kind=kOutput, calls=%fused_computation.33 | convolution fusion | flops 402653184 | bytes 2097152 | tf_op jit(solution)/shard_map/jcmb,jbo->cmjo/dot_general | solution.py:53
  77.6 0.9 copy.116
  78.5 1.6 copy.54
  80.1 2.8 %gather_fusion.1 = f32[8,2,64,256]{2,1,3,0:T(2,128)S(1)} fusion(f32[2,64,1280]{1,0,2:T(2,128)S(1)} %copy.54, s32[8]{0:T(128)S(1)} %get-tuple-element.26), kind=kCustom, calls=%fused_computation.1 | custom fusion | bytes 2097248 | tf_op jit(solution)/shard_map/vmap()/gather | solution.py:50
  82.9 2.9 %fusion.27 = f32[8,2,8,8,128]{4,3,2,1,0:T(8,128)S(1)} fusion(f32[8,2,64,256]{2,1,3,0:T(2,128)S(1)} %gather_fusion.1, bf16[4,8,256,128]{3,2,1,0:T(8,128)(2,1)} %param.4), kind=kOutput, calls=%fused_computation.32 | convolution fusion | flops 402653184 | bytes 2097152 | tf_op jit(solution)/shard_map/jcmb,jbo->cmjo/dot_general | solution.py:53
  85.8 0.9 copy.117
  86.6 1.6 copy.51
  88.2 2.8 %gather_fusion = f32[8,2,64,256]{2,1,3,0:T(2,128)S(1)} fusion(f32[2,64,1280]{1,0,2:T(2,128)S(1)} %copy.51, s32[8]{0:T(128)S(1)} %get-tuple-element.23), kind=kCustom, calls=%fused_computation | custom fusion | bytes 2097248 | tf_op jit(solution)/shard_map/vmap()/gather | solution.py:50
  91.0 2.9 %fusion.24 = f32[8,2,8,8,128]{4,3,2,1,0:T(8,128)S(1)} fusion(f32[8,2,64,256]{2,1,3,0:T(2,128)S(1)} %gather_fusion, bf16[4,8,256,128]{3,2,1,0:T(8,128)(2,1)} %param.4), kind=kOutput, calls=%fused_computation.31 | convolution fusion | flops 402653184 | bytes 2097152 | tf_op jit(solution)/shard_map/jcmb,jbo->cmjo/dot_general | solution.py:53
  93.9 0.9 copy.118
  94.7 1.6 copy.60
  96.3 2.8 %gather_fusion.3 = f32[8,2,64,256]{2,1,3,0:T(2,128)S(1)} fusion(f32[2,64,1280]{1,0,2:T(2,128)S(1)} %copy.60, s32[8]{0:T(128)S(1)} %get-tuple-element.24), kind=kCustom, calls=%fused_computation.3 | custom fusion | bytes 2097248 | tf_op jit(solution)/shard_map/vmap()/gather | solution.py:50
  99.1 0.0 copy-start.2
  99.2 3.0 %fusion.33 = f32[8,2,8,8,128]{4,3,2,1,0:T(8,128)S(1)} fusion(f32[8,2,64,256]{2,1,3,0:T(2,128)S(1)} %gather_fusion.3, bf16[4,8,256,128]{3,2,1,0:T(8,128)(2,1)} %param.4), kind=kOutput, calls=%fused_computation.34 | convolution fusion | flops 402653184 | bytes 2097152 | tf_op jit(solution)/shard_map/jcmb,jbo->cmjo/dot_general | solution.py:53
  102.3 3.6 %fusion.18 = f32[2,256,1024]{2,1,0:T(8,128)S(1)} fusion(f32[2,64,1024]{2,1,0:T(8,128)S(1)} %bitcast.143, f32[2,64,1024]{2,1,0:T(8,128)S(1)} %bitcast.140, f32[2,64,1024]{2,1,0:T(8,128)S(1)} %bitcast.141, f32[2,64,1024]{2,1,0:T(8,128)S(1)} %bitcast.142, f32[1,256,2,256]{3,1,2,0:T(8,128)S(1)} %copy-done.4, f32[1,256,2,256]{3,1,2,0:T(8,128)S(1)} %copy-done.3), kind=kOutput, calls=%fused_computation.27 | convolution fusion | flops 3223060480 | bytes 5242880 | tf_op jit(solution)/shard_map/dmck,ckr->dmr/dot_general | solution.py:94
  105.9 0.3 multiply_subtract_fusion
  106.2 0.2 maximum_bitcast_fusion.2
  106.5 1.6 copy.63
  108.1 52.6 %all_to_all.33 = f32[2,256,1,1024]{3,0,2,1:T(2,128)S(1)} all-to-all(f32[2,256,1,1024]{3,0,2,1:T(2,128)S(1)} %copy.63), channel_id=1, replica_groups=mesh['frames'=2,'az'=8,'rg'=2] {'az'}, dimensions={1} | all-to-all | bytes 4194304 | tf_op jit(solution)/shard_map/all_to_all | solution.py:107
  160.6 3.0 %fusion.21 = bf16[2,32,8,1024]{3,2,0,1:T(8,128)(2,1)S(1)} fusion(f32[2,8,32,1,1024]{4,0,2,1,3:T(2,128)S(1)} %bitcast.138, f32[1,8,2,8]{3,1,2,0:T(8,128)S(1)} %get-tuple-element.20, f32[1,8,2,8]{3,1,2,0:T(8,128)S(1)} %get-tuple-element.19), kind=kOutput, calls=%fused_computation.30 | convolution fusion | flops 101187840 | bytes 3146752 | tf_op jit(solution)/shard_map/dpck,cmkr->dmpr/dot_general | solution.py:104
  163.6 1.1 copy.66
  (15 shorter events, 0.1 us)
Async XLA Ops:
  5.7 55.5 %all-to-all-start = ((f32[2,32,8,1024]{3,1,0,2:T(8,128)}), f32[2,32,8,1024]{3,1,0,2:T(8,128)S(1)}, u32[]{:S(2)}, u32[]{:S(2)}) async-start(f32[2,32,8,1024]{3,1,0,2:T(8,128)} %copy.49), calls=%async_computation | async-start | bytes 4194304 | tf_op jit(solution)/shard_map/all_to_all | solution.py:83
  61.4 6.3 %copy-start.5 = (s32[4,16]{1,0:T(4,128)S(1)}, s32[4,16]{1,0:T(4,128)}, u32[]{:S(2)}) copy-start(s32[4,16]{1,0:T(4,128)} %param.5) | copy-start | bytes 772
  65.0 2.7 %collective-permute-start = (f32[2,256,128]{2,1,0:T(8,128)S(1)}, f32[2,256,128]{2,1,0:T(8,128)S(1)}, u32[]{:S(2)}, u32[]{:S(2)}) collective-permute-start(f32[2,256,128]{2,1,0:T(8,128)S(1)} %get-tuple-element.13), channel_id=1, source_target_pairs={{0,1},{2,3},{4,5},{6,7},{8,9},{10,11},{12,13},{14,15},{16,17},{18,... | collective-permute-start | bytes 786440 | tf_op jit(solution)/shard_map/ppermute | solution.py:19
  66.3 3.4 %collective-permute-start.1 = (f32[2,256,128]{2,1,0:T(8,128)S(1)}, f32[2,256,128]{2,1,0:T(8,128)S(1)}, u32[]{:S(2)}, u32[]{:S(2)}) collective-permute-start(f32[2,256,128]{2,1,0:T(8,128)S(1)} %get-tuple-element.14), channel_id=1, source_target_pairs={{1,0},{3,2},{5,4},{7,6},{9,8},{11,10},{13,12},{15,14},{17,16},{19,... | collective-permute-start | bytes 786440 | tf_op jit(solution)/shard_map/ppermute | solution.py:21
  99.1 3.1 %copy-start = (f32[8,2,8,8,128]{4,3,0,2,1:T(8,128)S(1)}, f32[8,2,8,8,128]{4,3,0,2,1:T(8,128)}, u32[]{:S(2)}) copy-start(f32[8,2,8,8,128]{4,3,0,2,1:T(8,128)} %copy.116) | copy-start | bytes 1572868
  99.1 3.1 %copy-start.1 = (f32[8,2,8,8,128]{4,3,0,2,1:T(8,128)S(1)}, f32[8,2,8,8,128]{4,3,0,2,1:T(8,128)}, u32[]{:S(2)}) copy-start(f32[8,2,8,8,128]{4,3,0,2,1:T(8,128)} %copy.117) | copy-start | bytes 1572868
  99.1 3.1 %copy-start.2 = (f32[8,2,8,8,128]{4,3,0,2,1:T(8,128)S(1)}, f32[8,2,8,8,128]{4,3,0,2,1:T(8,128)}, u32[]{:S(2)}) copy-start(f32[8,2,8,8,128]{4,3,0,2,1:T(8,128)} %copy.118) | copy-start | bytes 1572868
  99.1 3.1 %copy-start.3 = (f32[1,256,2,256]{3,1,2,0:T(8,128)S(1)}, f32[1,256,2,256]{3,1,2,0:T(8,128)}, u32[]{:S(2)}) copy-start(f32[1,256,2,256]{3,1,2,0:T(8,128)} %get-tuple-element.15) | copy-start | bytes 1572868
  99.2 3.1 %copy-start.4 = (f32[1,256,2,256]{3,1,2,0:T(8,128)S(1)}, f32[1,256,2,256]{3,1,2,0:T(8,128)}, u32[]{:S(2)}) copy-start(f32[1,256,2,256]{3,1,2,0:T(8,128)} %get-tuple-element.18) | copy-start | bytes 1572868
where the time goes:
time: 165 us
  blocking collectives  52.6 us (32%)
  waiting for transfers between devices  46 us (28%)
  local copies, waits for them, and re-layouts  25.9 us (16%)
  matrix products  24.1 us (15%)
  starting transfers between devices  9.85 us (6%)
  other arithmetic  5.92 us (4%)
    all_to_all x1, blocking collectives, body(): lax.all_to_all(unrolled, 'az', split_axis=1, concat_axis=2, tiled=True)  52.6 us
    all_to_all x1, waiting for transfers between devices, body(): lax.all_to_all(twisted, 'az', split_axis=2, concat_axis=1, tiled=True)  44 us
    dot_general x4, matrix products, stolt(): jnp.einsum('jcmb,jbo->cmjo', windows, weights[slab_index].astype(jnp.floa...  11.7 us
    gather x4, local copies, waits for them, and re-layouts, window_at(): return lax.dynamic_slice_in_dim(slab_data, start_bin, 256, 2)  11.2 us
    all_to_all x1, starting transfers between devices, body(): lax.all_to_all(twisted, 'az', split_axis=2, concat_axis=1, tiled=True)  7.25 us
    slice x5, local copies, waits for them, and re-layouts, stolt(): slab_source[:, slab_index * slab_rows:(slab_index + 1) * slab_rows, :]  6.67 us
    dot_general x1, matrix products, body(): jnp.einsum('dkcm,cmjr->dkjr', long_forward, lax.all_to_all(twisted, 'az',...  3.58 us
    dot_general x1, matrix products, body(): jnp.einsum('dmck,ckr->dmr', long_inverse, remapped, precision=lax.Precisi...  3.58 us
  transfers between devices with their start and end apart: 3, of which 2 were waited for; matrix products, arithmetic and copies ran while one was open for 3% of the time, Pallas kernels for 0%

commit v1 on v0

--- a/solution.py
+++ b/solution.py
@@ -104,7 +104,10 @@
     focused = jnp.einsum(
         "dpck,cmkr->dmpr",
         short_inverse,
-        lax.all_to_all(unrolled, "az", split_axis=1, concat_axis=2, tiled=True),
+        jnp.concatenate(
+            lax.all_to_all(jnp.stack(jnp.split(unrolled, lax.axis_size("az"), axis=1)), "az", 0, 0),
+            axis=2,
+        ),
         precision=lax.Precision.HIGHEST,
     )
     return focused.astype(jnp.bfloat16)

time: 165 us -> 164 us (level)
  no operation moved by 1% of the time
where the time goes in v1:
time: 164 us; the launch traced here: 163 us
  blocking collectives  52.6 us (32%)
  waiting for transfers between devices  46 us (28%)
  local copies, waits for them, and re-layouts  24.4 us (15%)
  matrix products  24.2 us (15%)
  starting transfers between devices  9.85 us (6%)
  other arithmetic  5.93 us (4%)
    all_to_all x1, blocking collectives, body(): lax.all_to_all(jnp.stack(jnp.split(unrolled, lax.axis_size('az'), axis=1)...  52.6 us
    all_to_all x1, waiting for transfers between devices, body(): lax.all_to_all(twisted, 'az', split_axis=2, concat_axis=1, tiled=True)  44 us
    dot_general x4, matrix products, stolt(): jnp.einsum('jcmb,jbo->cmjo', windows, weights[slab_index].astype(jnp.floa...  11.7 us
    gather x4, local copies, waits for them, and re-layouts, window_at(): return lax.dynamic_slice_in_dim(slab_data, start_bin, 256, 2)  11.2 us
    all_to_all x1, starting transfers between devices, body(): lax.all_to_all(twisted, 'az', split_axis=2, concat_axis=1, tiled=True)  7.25 us
    slice x5, local copies, waits for them, and re-layouts, stolt(): slab_source[:, slab_index * slab_rows:(slab_index + 1) * slab_rows, :]  6.67 us
    dot_general x1, matrix products, body(): jnp.einsum('dkcm,cmjr->dkjr', long_forward, lax.all_to_all(twisted, 'az',...  3.58 us
    dot_general x1, matrix products, body(): jnp.einsum('dmck,ckr->dmr', long_inverse, remapped, precision=lax.Precisi...  3.58 us
  transfers between devices with their start and end apart: 3, of which 2 were waited for; matrix products, arithmetic and copies ran while one was open for 3% of the time, Pallas kernels for 0%

profile of v1, /device:TPU:0, one launch (start us, length us, event | category | flops | bytes accessed | tf_op | source)
XLA Modules:
  0.0 163.4 jit_solution(396282825998567294)
XLA Ops:
  0.0 0.1 cosine_multiply_fusion.1
  0.1 0.1 broadcast_multiply_fusion.3
  0.1 0.1 fusion.95
  0.2 0.2 fusion.86
  0.4 2.3 %convolution_bitcast_fusion.1 = f32[2,32,8,1024]{3,2,1,0:T(8,128)S(1)} fusion(bf16[2,32,8,1024]{3,2,1,0:T(8,128)(2,1)} %param.3, f32[1,8,2,8]{3,1,2,0:T(8,128)S(1)} %get-tuple-element.21, f32[1,8,2,8]{3,1,2,0:T(8,128)S(1)} %get-tuple-element.22), kind=kOutput, calls=%fused_computation.28 | convolution fusion | flops 100663552 | bytes 3146752 | tf_op jit(solution)/shard_map/dkcp,cmpr->dmkr/dot_general | solution.py:71
  2.6 0.3 multiply_subtract_fusion.1
  2.9 0.2 pad_maximum_fusion.1
  3.2 2.6 %copy.32 = f32[2,32,8,1024]{3,1,0,2:T(8,128)} copy(f32[2,32,8,1024]{3,2,1,0:T(8,128)S(1)} %pad_maximum_fusion.1) | data formatting | bytes 4194304 | tf_op jit(solution)/shard_map/stack | solution.py:78
  5.7 7.3 %all-to-all-start = ((f32[2,32,8,1024]{3,1,0,2:T(8,128)}), f32[2,32,8,1024]{3,1,0,2:T(8,128)S(1)}, u32[]{:S(2)}, u32[]{:S(2)}) async-start(f32[2,32,8,1024]{3,1,0,2:T(8,128)} %copy.32), calls=%async_computation | async-start | bytes 4194304 | tf_op jit(solution)/shard_map/all_to_all | solution.py:83
  13.0 0.1 fusion.111
  13.0 1.0 fusion.71
  14.0 1.1 cosine_multiply_fusion
  15.1 1.0 broadcast_multiply_fusion.1
  16.1 1.2 fusion.45
  17.2 44.0 %all-to-all-done = f32[2,32,8,1024]{3,1,0,2:T(8,128)S(1)} async-done(((f32[2,32,8,1024]{3,1,0,2:T(8,128)}), f32[2,32,8,1024]{3,1,0,2:T(8,128)S(1)}, u32[]{:S(2)}, u32[]{:S(2)}) %all-to-all-start) | async-done | bytes 2097184 | tf_op jit(solution)/shard_map/all_to_all | solution.py:83
  61.2 0.1 copy.33
  61.4 0.0 copy-start.5
  61.4 3.6 %convolution_bitcast_fusion = f32[2,256,1024]{2,1,0:T(8,128)S(1)} fusion(f32[2,256,1024,1]{2,1,0,3:T(8,128)S(1)} %bitcast.162, f32[1,256,2,256]{3,1,2,0:T(8,128)S(1)} %get-tuple-element.16, f32[1,256,2,256]{3,1,2,0:T(8,128)S(1)} %get-tuple-element.17), kind=kOutput, calls=%fused_computation.27 | convolution fusion | flops 3221487616 | bytes 5242880 | tf_op jit(solution)/shard_map/dkcm,cmjr->dkjr/dot_general | solution.py:80
  65.0 1.3 collective-permute-start
  66.3 1.3 collective-permute-start.1
  67.6 0.1 multiply_add_fusion.2
  67.7 0.0 collective-permute-done
  67.8 2.0 %collective-permute-done.1 = f32[2,256,128]{2,1,0:T(8,128)S(1)} collective-permute-done((f32[2,256,128]{2,1,0:T(8,128)S(1)}, f32[2,256,128]{2,1,0:T(8,128)S(1)}, u32[]{:S(2)}, u32[]{:S(2)}) %collective-permute-start.1) | collective-permute-done | bytes 262176 | tf_op jit(solution)/shard_map/ppermute | solution.py:21
  69.8 0.2 pad_maximum_fusion
  70.0 1.3 fusion.117
  71.3 0.7 copy.40
  71.9 2.8 %gather_fusion.2 = f32[8,2,64,256]{2,1,3,0:T(2,128)S(1)} fusion(f32[2,64,1280]{1,0,2:T(2,128)S(1)} %copy.40, s32[8]{0:T(128)S(1)} %get-tuple-element.25), kind=kCustom, calls=%fused_computation.2 | custom fusion | bytes 2097248 | tf_op jit(solution)/shard_map/vmap()/gather | solution.py:50
  74.7 2.9 %fusion.29 = f32[8,2,8,8,128]{4,3,2,1,0:T(8,128)S(1)} fusion(f32[8,2,64,256]{2,1,3,0:T(2,128)S(1)} %gather_fusion.2, bf16[4,8,256,128]{3,2,1,0:T(8,128)(2,1)} %param.4), kind=kOutput, calls=%fused_computation.32 | convolution fusion | flops 402653184 | bytes 2097152 | tf_op jit(solution)/shard_map/jcmb,jbo->cmjo/dot_general | solution.py:53
  77.6 0.9 copy.95
  78.5 1.6 copy.37
  80.1 2.8 %gather_fusion.1 = f32[8,2,64,256]{2,1,3,0:T(2,128)S(1)} fusion(f32[2,64,1280]{1,0,2:T(2,128)S(1)} %copy.37, s32[8]{0:T(128)S(1)} %get-tuple-element.26), kind=kCustom, calls=%fused_computation.1 | custom fusion | bytes 2097248 | tf_op jit(solution)/shard_map/vmap()/gather | solution.py:50
  82.9 2.9 %fusion.26 = f32[8,2,8,8,128]{4,3,2,1,0:T(8,128)S(1)} fusion(f32[8,2,64,256]{2,1,3,0:T(2,128)S(1)} %gather_fusion.1, bf16[4,8,256,128]{3,2,1,0:T(8,128)(2,1)} %param.4), kind=kOutput, calls=%fused_computation.31 | convolution fusion | flops 402653184 | bytes 2097152 | tf_op jit(solution)/shard_map/jcmb,jbo->cmjo/dot_general | solution.py:53
  85.8 0.9 copy.96
  86.6 1.6 copy.34
  88.2 2.8 %gather_fusion = f32[8,2,64,256]{2,1,3,0:T(2,128)S(1)} fusion(f32[2,64,1280]{1,0,2:T(2,128)S(1)} %copy.34, s32[8]{0:T(128)S(1)} %get-tuple-element.23), kind=kCustom, calls=%fused_computation | custom fusion | bytes 2097248 | tf_op jit(solution)/shard_map/vmap()/gather | solution.py:50
  91.0 2.9 %fusion.23 = f32[8,2,8,8,128]{4,3,2,1,0:T(8,128)S(1)} fusion(f32[8,2,64,256]{2,1,3,0:T(2,128)S(1)} %gather_fusion, bf16[4,8,256,128]{3,2,1,0:T(8,128)(2,1)} %param.4), kind=kOutput, calls=%fused_computation.30 | convolution fusion | flops 402653184 | bytes 2097152 | tf_op jit(solution)/shard_map/jcmb,jbo->cmjo/dot_general | solution.py:53
  93.9 0.9 copy.97
  94.7 1.6 copy.43
  96.3 2.8 %gather_fusion.3 = f32[8,2,64,256]{2,1,3,0:T(2,128)S(1)} fusion(f32[2,64,1280]{1,0,2:T(2,128)S(1)} %copy.43, s32[8]{0:T(128)S(1)} %get-tuple-element.24), kind=kCustom, calls=%fused_computation.3 | custom fusion | bytes 2097248 | tf_op jit(solution)/shard_map/vmap()/gather | solution.py:50
  99.1 0.0 copy-start.2
  99.2 3.0 %fusion.32 = f32[8,2,8,8,128]{4,3,2,1,0:T(8,128)S(1)} fusion(f32[8,2,64,256]{2,1,3,0:T(2,128)S(1)} %gather_fusion.3, bf16[4,8,256,128]{3,2,1,0:T(8,128)(2,1)} %param.4), kind=kOutput, calls=%fused_computation.33 | convolution fusion | flops 402653184 | bytes 2097152 | tf_op jit(solution)/shard_map/jcmb,jbo->cmjo/dot_general | solution.py:53
  102.3 0.0 copy-done
  102.3 3.6 %fusion.17 = f32[2,256,1024]{2,1,0:T(8,128)S(1)} fusion(f32[2,64,1024]{2,1,0:T(8,128)S(1)} %bitcast.166, f32[2,64,1024]{2,1,0:T(8,128)S(1)} %bitcast.163, f32[2,64,1024]{2,1,0:T(8,128)S(1)} %bitcast.164, f32[2,64,1024]{2,1,0:T(8,128)S(1)} %bitcast.165, f32[1,256,2,256]{3,1,2,0:T(8,128)S(1)} %copy-done.4, f32[1,256,2,256]{3,1,2,0:T(8,128)S(1)} %copy-done.3), kind=kOutput, calls=%fused_computation.26 | convolution fusion | flops 3223060480 | bytes 5242880 | tf_op jit(solution)/shard_map/dmck,ckr->dmr/dot_general | solution.py:94
  105.9 0.3 multiply_subtract_fusion
  106.2 0.2 maximum_bitcast_fusion.2
  106.7 52.6 %all_to_all.20 = f32[8,2,32,1,1024]{4,2,1,3,0:T(8,128)S(1)} all-to-all(f32[8,2,32,1,1024]{4,2,1,3,0:T(8,128)S(1)} %fusion.58), channel_id=1, replica_groups=mesh['frames'=2,'az'=8,'rg'=2] {'az'}, dimensions={0} | all-to-all | bytes 4194304 | tf_op jit(solution)/shard_map/all_to_all | solution.py:108
  159.2 3.1 %fusion.20 = bf16[2,32,8,1024]{3,2,0,1:T(8,128)(2,1)S(1)} fusion(f32[2,32,8,1024,1]{3,1,0,2,4:T(8,128)S(1)} %bitcast.161, f32[1,8,2,8]{3,1,2,0:T(8,128)S(1)} %get-tuple-element.20, f32[1,8,2,8]{3,1,2,0:T(8,128)S(1)} %get-tuple-element.19), kind=kOutput, calls=%fused_computation.29 | convolution fusion | flops 101187840 | bytes 3146752 | tf_op jit(solution)/shard_map/dpck,cmkr->dmpr/dot_general | solution.py:104
  162.3 1.1 copy.47
  (22 shorter events, 0.3 us)
Async XLA Ops:
  5.7 55.5 %all-to-all-start = ((f32[2,32,8,1024]{3,1,0,2:T(8,128)}), f32[2,32,8,1024]{3,1,0,2:T(8,128)S(1)}, u32[]{:S(2)}, u32[]{:S(2)}) async-start(f32[2,32,8,1024]{3,1,0,2:T(8,128)} %copy.32), calls=%async_computation | async-start | bytes 4194304 | tf_op jit(solution)/shard_map/all_to_all | solution.py:83
  61.4 6.3 %copy-start.5 = (s32[4,16]{1,0:T(4,128)S(1)}, s32[4,16]{1,0:T(4,128)}, u32[]{:S(2)}) copy-start(s32[4,16]{1,0:T(4,128)} %param.5) | copy-start | bytes 772
  65.0 2.7 %collective-permute-start = (f32[2,256,128]{2,1,0:T(8,128)S(1)}, f32[2,256,128]{2,1,0:T(8,128)S(1)}, u32[]{:S(2)}, u32[]{:S(2)}) collective-permute-start(f32[2,256,128]{2,1,0:T(8,128)S(1)} %get-tuple-element.13), channel_id=1, source_target_pairs={{0,1},{2,3},{4,5},{6,7},{8,9},{10,11},{12,13},{14,15},{16,17},{18,... | collective-permute-start | bytes 786440 | tf_op jit(solution)/shard_map/ppermute | solution.py:19
  66.3 3.4 %collective-permute-start.1 = (f32[2,256,128]{2,1,0:T(8,128)S(1)}, f32[2,256,128]{2,1,0:T(8,128)S(1)}, u32[]{:S(2)}, u32[]{:S(2)}) collective-permute-start(f32[2,256,128]{2,1,0:T(8,128)S(1)} %get-tuple-element.14), channel_id=1, source_target_pairs={{1,0},{3,2},{5,4},{7,6},{9,8},{11,10},{13,12},{15,14},{17,16},{19,... | collective-permute-start | bytes 786440 | tf_op jit(solution)/shard_map/ppermute | solution.py:21
  99.1 3.1 %copy-start = (f32[8,2,8,8,128]{4,3,0,2,1:T(8,128)S(1)}, f32[8,2,8,8,128]{4,3,0,2,1:T(8,128)}, u32[]{:S(2)}) copy-start(f32[8,2,8,8,128]{4,3,0,2,1:T(8,128)} %copy.95) | copy-start | bytes 1572868
  99.1 3.1 %copy-start.1 = (f32[8,2,8,8,128]{4,3,0,2,1:T(8,128)S(1)}, f32[8,2,8,8,128]{4,3,0,2,1:T(8,128)}, u32[]{:S(2)}) copy-start(f32[8,2,8,8,128]{4,3,0,2,1:T(8,128)} %copy.96) | copy-start | bytes 1572868
  99.1 3.1 %copy-start.2 = (f32[8,2,8,8,128]{4,3,0,2,1:T(8,128)S(1)}, f32[8,2,8,8,128]{4,3,0,2,1:T(8,128)}, u32[]{:S(2)}) copy-start(f32[8,2,8,8,128]{4,3,0,2,1:T(8,128)} %copy.97) | copy-start | bytes 1572868
  99.1 3.1 %copy-start.3 = (f32[1,256,2,256]{3,1,2,0:T(8,128)S(1)}, f32[1,256,2,256]{3,1,2,0:T(8,128)}, u32[]{:S(2)}) copy-start(f32[1,256,2,256]{3,1,2,0:T(8,128)} %get-tuple-element.15) | copy-start | bytes 1572868
  99.2 3.1 %copy-start.4 = (f32[1,256,2,256]{3,1,2,0:T(8,128)S(1)}, f32[1,256,2,256]{3,1,2,0:T(8,128)}, u32[]{:S(2)}) copy-start(f32[1,256,2,256]{3,1,2,0:T(8,128)} %get-tuple-element.18) | copy-start | bytes 1572868
